TPU v7x, 128 devices: a whole 4x4x4 slice. The times are simulated.
128 devices in a mesh: req: 64 (over z, y, x_hi, core), tp: 2 (over x_lo).
Axes of the slice: x: 4 (x_hi: 2, x_lo: 2; x = x_hi * 2 + x_lo), y: 4, z: 4, core: 2. Of those that a mesh axis runs over, the one named last changes fastest.
Arguments:
- arrivals: bfloat16 [32768, 2048], P('req', 'tp'), may hold values from -16 to 16
- packing: int32 [256], P('req'), may hold values from 0 to 255, as said below
- segment_ids: int32 [32768], P('req'), may hold values from 0 to 32767, as said below
- page_table: int32 [256], P('req'), may hold values from 0 to 255, as said below
- attn_gain: float32 [2048], replicated, may hold values from 0.25 to 1.75
- w_query: bfloat16 [2048, 2048], P(None, 'tp'), may hold values from -0.015625 to 0.015625
- w_key: bfloat16 [2048, 2048], P(None, 'tp'), may hold values from -0.125 to 0.125
- w_value: bfloat16 [2048, 2048], P(None, 'tp'), may hold values from -0.125 to 0.125
- w_out: bfloat16 [2048, 2048], P('tp'), may hold values from -0.1875 to 0.1875
- rel_bias: float32 [32, 32], P(None, 'tp'), may hold values from -4 to 260
- final_gain: float32 [2048], replicated, may hold values from 0.25 to 1.75
- cross_key: bfloat16 [2048, 2048], P(None, 'tp'), may hold values from -0.125 to 0.125
- cross_value: bfloat16 [2048, 2048], P(None, 'tp'), may hold values from -0.125 to 0.125
Outputs:
- hidden: bfloat16 [32768, 2048], P('req', 'tp')
- cache: bfloat16 [256, 128, 2, 2048], P('req', None, None, 'tp')
Inputs may be any that keep to these rules, and one draw needn't show every extreme that they name: `packing`: A permutation of the block numbers; the entries of index r of req name, by their quotient by 4, the indices r XOR m for every m below 4, each exactly 1 times. `segment_ids`: Non-decreasing; every segment lies within the 512 tokens of one index of req and has at most 256 tokens; some index holds one of exactly 256. `page_table`: A permutation of the slots; the entries of index r of req name, by their quotient by 4, the indices r XOR m for every m below 4, each exactly 1 times; slot s lies on index s // 4 of req.
All inputs are finite; a program needn't handle non-finite values.
Results may differ from a plain program's by a relative error of at most 0.01.
Values may be sent and summed in bfloat16 or wider, within the bound.
No kernel may reach another device: no remote copies, remote signals or barrier semaphores. Data moves between devices by JAX's collectives and lax.ppermute only.
A program may use at most 256 MiB of HBM per device.

v0:
```python
import jax
import jax.numpy as jnp
from jax import lax
from jax.experimental import pallas as pl
from jax.experimental.pallas import tpu as pltpu
from jax.sharding import PartitionSpec as P

PAGE = 128
HEAD_DIM = 64
SPREAD = 640
TURN = 1024
GROUP = 256
MIB = 1 << 20

epsilon = 1e-06
far_steps = (12, 16, 23, 32, 46, 64, 91)
NEG = float("-inf")


def exchange(block, mask, flip):
    count = lax.axis_size("req")
    pairs = [(r * 2 + t, (r ^ mask) * 2 + (t ^ flip)) for r in range(count) for t in range(2)]
    return lax.ppermute(block, ("req", "tp"), pairs)


def buckets(offsets):
    distance = jnp.abs(offsets)
    far_bucket = 8 + sum((distance >= threshold).astype(jnp.int32) for threshold in far_steps)
    bucket_ids = jnp.where(distance < 8, distance, far_bucket)
    return bucket_ids + jnp.where(offsets > 0, 16, 0).astype(jnp.int32)


def any_spec():
    return pl.BlockSpec(memory_space=pl.ANY)


def smem_spec():
    return pl.BlockSpec(memory_space=pltpu.SMEM)


def hbm_spec():
    return pl.BlockSpec(memory_space=pltpu.HBM)


def vmem_spec():
    return pl.BlockSpec(memory_space=pltpu.VMEM)


def params(mib, grid_rank=1):
    return pltpu.CompilerParams(
        dimension_semantics=("arbitrary",) * grid_rank, vmem_limit_bytes=mib * MIB
    )


def lane_order(packing, page_table, arrived, me):
    def body(packing_ref, table_ref, me_ref, rows_ref, *rest):
        row_outs, tag_outs, page_out = rest[:4], rest[4:8], rest[8]
        me_here = me_ref[0]
        for m in range(4):
            source = jnp.int32(0)
            pack_slot = jnp.int32(0)
            page = jnp.int32(0)
            page_slot = jnp.int32(0)
            for j in range(4):
                hit = ((packing_ref[j] // 4) ^ me_here) == m
                source = jnp.where(hit, j, source)
                pack_slot = jnp.where(hit, packing_ref[j] % 4, pack_slot)
                owned = ((table_ref[j] // 4) ^ me_here) == m
                page = jnp.where(owned, j, page)
                page_slot = jnp.where(owned, table_ref[j] % 4, page_slot)
            tag_outs[m][0] = pack_slot
            tag_outs[m][1] = page_slot
            page_out[m] = page
            row_outs[m][...] = rows_ref[source]

    shape = jax.ShapeDtypeStruct(arrived.shape[1:], arrived.dtype)
    outs = pl.pallas_call(
        body,
        grid_spec=pltpu.PrefetchScalarGridSpec(
            num_scalar_prefetch=3,
            grid=(),
            in_specs=[vmem_spec()],
            out_specs=[vmem_spec()] * 4 + [smem_spec()] * 5,
        ),
        out_shape=[shape] * 4
        + [jax.ShapeDtypeStruct((2,), jnp.int32)] * 4
        + [jax.ShapeDtypeStruct((4,), jnp.int32)],
        compiler_params=pltpu.CompilerParams(vmem_limit_bytes=8 * MIB),
        name="lane_order",
    )(packing, page_table, me, arrived)
    return outs[:4], outs[4:8], outs[8]


def bias_tiles(rel_bias):
    table = jnp.transpose(rel_bias)
    heads = table.shape[0]

    def body(table_ref, out_ref):
        lane = lax.broadcasted_iota(jnp.int32, (heads, TURN), 1)
        bucket_ids = buckets(jnp.where(lane < SPREAD, lane - 2 * PAGE, lane - 2 * PAGE - TURN))
        values = table_ref[...]
        row = jnp.zeros((heads, TURN), jnp.float32)
        for b in range(table.shape[1]):
            row = jnp.where(bucket_ids == b, values[:, b : b + 1], row)
        for h in range(heads):
            wide = jnp.broadcast_to(row[h : h + 1, :], (PAGE, TURN))
            turned = pltpu.roll(wide, 0, 1, stride=1, stride_axis=0)
            out_ref[h * PAGE : (h + 1) * PAGE, :] = turned[:, :SPREAD]

    return pl.pallas_call(
        body,
        out_shape=jax.ShapeDtypeStruct((heads * PAGE, SPREAD), jnp.float32),
        compiler_params=pltpu.CompilerParams(vmem_limit_bytes=16 * MIB),
        cost_estimate=pl.CostEstimate(flops=0, transcendentals=0, bytes_accessed=48 * MIB),
        name="bias_tiles",
    )(table)


def normalize(side, first_refs, second_refs, gain_ref, out_ref):
    half = first_refs[0].shape[-1]
    for i, (first_ref, second_ref) in enumerate(zip(first_refs, second_refs)):
        first = first_ref[...].astype(jnp.float32)
        second = second_ref[...].astype(jnp.float32)
        total = jnp.sum(first * first, axis=-1, keepdims=True) + jnp.sum(
            second * second, axis=-1, keepdims=True
        )
        scale = lax.rsqrt(total * (1.0 / (2 * half)) + epsilon)
        left = jnp.where(side == 0, first, second)
        right = jnp.where(side == 0, second, first)
        rows = slice(i * PAGE, (i + 1) * PAGE)
        out_ref[rows, :half] = (left * scale * gain_ref[:, :half]).astype(jnp.bfloat16)
        out_ref[rows, half:] = (right * scale * gain_ref[:, half:]).astype(jnp.bfloat16)


def project(part, first, second, side, gain, weights, earlier):
    half = first[0].shape[1]
    columns = weights[0].shape[1]

    starts = range(0, columns, GROUP)

    def body(side_ref, f0, f1, s0, s1, gain_ref, wq, wk, wv, *rest):
        q_out, k_out, v_out, own_out, normed, held, sems = rest[-7:]
        copies = []
        for n, start in enumerate(starts):
            here = slice(start, start + GROUP)
            for i, w_ref in enumerate((wq, wk, wv)):
                copy = pltpu.make_async_copy(w_ref.at[:, here], held.at[i, :, here], sems.at[n, i])
                copy.start()
                copies.append(copy)
        normalize(side_ref[0], (f0, f1), (s0, s1), gain_ref, normed)
        own_out[0] = f0[...]
        own_out[1] = f1[...]
        for n, start in enumerate(starts):
            here = slice(start, start + GROUP)
            for i, out in enumerate((q_out, k_out, v_out)):
                copies[3 * n + i].wait()
                product = jnp.dot(normed[...], held[i, :, here], preferred_element_type=jnp.float32)
                out[:, :, here] = product.astype(jnp.bfloat16).reshape(2, PAGE, GROUP)

    out = pl.BlockSpec((2, PAGE, columns), lambda n, s: (part, 0, 0))
    own = pl.BlockSpec((2, PAGE, half), lambda n, s: (part, 0, 0))
    shape = jax.ShapeDtypeStruct((4, PAGE, columns), jnp.bfloat16)
    return pl.pallas_call(
        body,
        grid_spec=pltpu.PrefetchScalarGridSpec(
            num_scalar_prefetch=1,
            grid=(1,),
            in_specs=[vmem_spec()] * 5 + [hbm_spec()] * 3 + [any_spec()] * len(earlier),
            out_specs=[out, out, out, own],
            scratch_shapes=[
                pltpu.VMEM((2 * PAGE, 2 * half), jnp.bfloat16),
                pltpu.VMEM((3, 2 * half, columns), jnp.bfloat16),
                pltpu.SemaphoreType.DMA((len(starts), 3)),
            ],
        ),
        out_shape=[shape, shape, shape, jax.ShapeDtypeStruct((4, PAGE, half), jnp.bfloat16)],
        input_output_aliases={9 + i: i for i in range(len(earlier))},
        compiler_params=params(24),
        cost_estimate=pl.CostEstimate(
            flops=2 * 2 * PAGE * 2 * half * 3 * columns,
            transcendentals=0,
            bytes_accessed=2 * 2 * half * columns,
        ),
        name="project",
    )(side, *first, *second, gain, *weights, *earlier)


def lane_of(meta, block):
    lane = jnp.int32(0)
    for m in range(1, 4):
        lane = jnp.where(meta[2 * m] == block, m, lane)
    return lane


def attend(lanes, meta, segments, side, queries, keys_local, values_local, w_out, bias):
    inner = w_out.shape[0]
    width = w_out.shape[1]
    pair = 2 * HEAD_DIM
    pairs = inner // pair
    tall = 2 * PAGE

    def body(meta_ref, seg_ref, side_ref, q_ref, k_ref, v_ref, rows_ref, w_ref, bias_ref,
             own_out, send_out, ctx, m_sc, a_sc, seg_sc):
        low = lax.broadcasted_iota(jnp.int32, (PAGE, pair), 1) < HEAD_DIM
        ones = jnp.ones((PAGE, PAGE), jnp.bfloat16)

        def hidden_pairs(i, key_block):
            same = seg_sc[i] == rows_ref[pl.ds(key_block, 1), :]
            return jnp.where(same, 0.0, NEG).astype(jnp.float32)

        def scores(at, key_at, hide, tile, p):
            cols = slice(p * pair, (p + 1) * pair)
            q = q_ref[at, :, cols]
            zero = jnp.zeros_like(q)
            stacked = jnp.concatenate([jnp.where(low, q, zero), jnp.where(low, zero, q)], axis=0)
            s = lax.dot_general(
                stacked, k_ref[key_at, :, cols], (((1,), (1,)), ((), ())),
                preferred_element_type=jnp.float32,
            )
            s = s + bias_ref[p * tall : (p + 1) * tall, tile]
            return s + jnp.concatenate([hide, hide], axis=0)

        def weighted(weights, key_at, p):
            wide = jnp.concatenate([v_ref[key_at, :, p * pair : (p + 1) * pair], ones], axis=1)
            return jnp.dot(weights, wide, preferred_element_type=jnp.float32)

        places = []
        for i, m in enumerate(lanes):
            block = meta_ref[8 + m]
            row = rows_ref[pl.ds(block, 1), :]
            seg_sc[i] = jnp.transpose(jnp.broadcast_to(row, (PAGE, PAGE)))
            places.append((block, lane_of(meta_ref, block)))
        for i, (block, at) in enumerate(places):
            hide = hidden_pairs(i, block)
            for p in range(pairs):
                s = scores(at, at, hide, slice(2 * PAGE, 3 * PAGE), p)
                top = jnp.max(s, axis=-1, keepdims=True)
                weights = jnp.exp(s - top).astype(jnp.bfloat16)
                m_sc[i, p] = jnp.broadcast_to(top, (tall, PAGE))
                a_sc[i, p] = weighted(weights, at, p)

        @pl.loop(0, 8)
        def _(turn):
            i = turn // 4
            slot = turn % 4
            delta = jnp.where(slot < 2, slot - 2, slot - 1)
            block = jnp.where(i == 0, places[0][0], places[1][0])
            at = jnp.where(i == 0, places[0][1], places[1][1])
            key_block = block + delta
            last = jnp.minimum(block, key_block) * PAGE + PAGE - 1
            first = jnp.maximum(block, key_block) * PAGE
            top_index = 4 * PAGE - 1
            joined = seg_ref[jnp.clip(last, 0, top_index)] == seg_ref[jnp.clip(first, 0, top_index)]
            inside = jnp.logical_and(key_block >= 0, key_block < 4)

            @pl.when(jnp.logical_and(inside, joined))
            def _():
                key_at = lane_of(meta_ref, key_block)
                hide = hidden_pairs(i, key_block)
                tile = pl.ds(pl.multiple_of((delta + 2) * PAGE, PAGE), PAGE)
                for p in range(pairs):
                    s = scores(at, key_at, hide, tile, p)
                    before = m_sc[i, p]
                    top = jnp.maximum(before, jnp.max(s, axis=-1, keepdims=True))
                    fade = jnp.exp(before - top)
                    weights = jnp.exp(s - top).astype(jnp.bfloat16)
                    m_sc[i, p] = top
                    a_sc[i, p] = a_sc[i, p] * jnp.concatenate([fade, fade], axis=1) + weighted(
                        weights, key_at, p
                    )

        for i in range(2):
            for p in range(pairs):
                mixed = jnp.where(low, a_sc[i, p, :PAGE, :pair], a_sc[i, p, PAGE:, :pair])
                total = jnp.where(low, a_sc[i, p, :PAGE, pair:], a_sc[i, p, PAGE:, pair:])
                ctx[i * PAGE : (i + 1) * PAGE, p * pair : (p + 1) * pair] = (mixed / total).astype(
                    jnp.bfloat16
                )

        half = width // 2
        for out, here in ((own_out, side_ref[0]), (send_out, 1 - side_ref[0])):
            for start in range(0, half, GROUP):
                at = pl.multiple_of(here * half + start, GROUP)
                out[:, start : start + GROUP] = jnp.dot(
                    ctx[...], w_ref[:, pl.ds(at, GROUP)], preferred_element_type=jnp.float32
                ).astype(jnp.bfloat16)

    shape = jax.ShapeDtypeStruct((tall, width // 2), jnp.bfloat16)
    return pl.pallas_call(
        body,
        grid_spec=pltpu.PrefetchScalarGridSpec(
            num_scalar_prefetch=3,
            grid=(1,),
            in_specs=[vmem_spec()] * 6,
            out_specs=[vmem_spec()] * 2,
            scratch_shapes=[
                pltpu.VMEM((tall, inner), jnp.bfloat16),
                pltpu.VMEM((2, pairs, tall, PAGE), jnp.float32),
                pltpu.VMEM((2, pairs, tall, pair + PAGE), jnp.float32),
                pltpu.VMEM((2, PAGE, PAGE), jnp.int32),
            ],
        ),
        out_shape=[shape, shape],
        compiler_params=params(24),
        cost_estimate=pl.CostEstimate(
            flops=2 * tall * inner * width * 2,
            transcendentals=tall * 512 * 16,
            bytes_accessed=10 * MIB,
        ),
        name="attend",
    )(meta, segments, side, queries, keys_local, values_local,
      segments.reshape(4, PAGE), w_out, bias)


def residual(lanes, meta, own, received, packed, earlier):
    half = own.shape[1]

    def page(i, meta_ref):
        return jnp.where(i == 0, meta_ref[8 + lanes[0]], meta_ref[8 + lanes[1]])

    def body(meta_ref, own_ref, got_ref, packed_ref, *rest):
        out, first, second = rest[-3:]
        added = own_ref[...].astype(jnp.float32) + got_ref[...].astype(jnp.float32)
        value = (packed_ref[0].astype(jnp.float32) + added).astype(jnp.bfloat16)
        out[0] = value

        @pl.when(pl.program_id(0) == 0)
        def _():
            first[...] = value

        @pl.when(pl.program_id(0) == 1)
        def _():
            second[...] = value

    block = pl.BlockSpec((PAGE, half), lambda i, s: (i, 0))
    alone = pl.BlockSpec((PAGE, half), lambda i, s: (0, 0))
    shape = jax.ShapeDtypeStruct((PAGE, half), jnp.bfloat16)
    return pl.pallas_call(
        body,
        grid_spec=pltpu.PrefetchScalarGridSpec(
            num_scalar_prefetch=1,
            grid=(2,),
            in_specs=[
                block,
                block,
                pl.BlockSpec((1, PAGE, half), lambda i, s: (lane_of(s, page(i, s)), 0, 0)),
            ]
            + [any_spec()] * len(earlier),
            out_specs=[pl.BlockSpec((1, PAGE, half), lambda i, s: (page(i, s), 0, 0)), alone, alone],
        ),
        out_shape=[jax.ShapeDtypeStruct((4, PAGE, half), jnp.bfloat16), shape, shape],
        input_output_aliases={4 + i: i for i in range(len(earlier))},
        compiler_params=params(8),
        name="residual",
    )(meta, own, received, packed, *earlier)


def cross(lanes, meta, side, first, second, gain, cross_key, cross_value, earlier):
    half = first[0].shape[1]
    columns = cross_key.shape[1]

    def body(meta_ref, side_ref, f0, f1, s0, s1, gain_ref, wk, wv, *rest):
        out, final, pages, sems = rest[-4:]
        normalize(side_ref[0], (f0, f1), (s0, s1), gain_ref, final)
        copies = []
        for start in range(0, columns, GROUP):
            here = slice(start, start + GROUP)
            keys_part, values_part = (
                jnp.dot(final[...], w_ref[:, here], preferred_element_type=jnp.float32).astype(jnp.bfloat16)
                for w_ref in (wk, wv)
            )
            both = jnp.stack([keys_part, values_part], axis=1)
            for i, m in enumerate(lanes):
                pages[i, :, :, here] = both[i * PAGE : (i + 1) * PAGE]
        for i, m in enumerate(lanes):
            copy = pltpu.make_async_copy(pages.at[i], out.at[meta_ref[2 * m + 1]], sems.at[i])
            copy.start()
            copies.append(copy)
        for copy in copies:
            copy.wait()

    return pl.pallas_call(
        body,
        grid_spec=pltpu.PrefetchScalarGridSpec(
            num_scalar_prefetch=2,
            grid=(1,),
            in_specs=[vmem_spec()] * 7 + [any_spec()] * len(earlier),
            out_specs=any_spec(),
            scratch_shapes=[
                pltpu.VMEM((2 * PAGE, 2 * half), jnp.bfloat16),
                pltpu.VMEM((2, PAGE, 2, columns), jnp.bfloat16),
                pltpu.SemaphoreType.DMA((2,)),
            ],
        ),
        out_shape=jax.ShapeDtypeStruct((4, PAGE, 2, columns), jnp.bfloat16),
        input_output_aliases={9: 0} if earlier else {},
        compiler_params=params(24),
        cost_estimate=pl.CostEstimate(
            flops=2 * 2 * PAGE * 2 * half * 2 * columns,
            transcendentals=0,
            bytes_accessed=2 * 2 * half * columns * 2,
        ),
        name="cross",
    )(meta, side, *first, *second, gain, cross_key, cross_value, *earlier)


def near(rows):
    other_zero = exchange(rows[0], 0, 1)
    own_one = exchange(rows[1], 1, 0)
    other_one = exchange(rows[1], 1, 1)
    return (rows[0], own_one), (other_zero, other_one)


def far(rows):
    other_two = exchange(rows[0], 2, 1)
    other_three = exchange(rows[1], 3, 1)
    own_two = exchange(other_two, 0, 1)
    own_three = exchange(other_three, 0, 1)
    return (own_two, own_three), (other_two, other_three)


def shards(
    arrivals,
    packing,
    segment_ids,
    page_table,
    attn_gain,
    w_query,
    w_key,
    w_value,
    w_out,
    rel_bias,
    final_gain,
    cross_key,
    cross_value,
):
    token_count, half = arrivals.shape
    me = lax.axis_index("req").astype(jnp.int32).reshape(1)
    side = lax.axis_index("tp").astype(jnp.int32).reshape(1)
    rows, tags, pages = lane_order(packing, page_table, arrivals.reshape(4, PAGE, half), me)
    far_own, far_other = far(rows[2:])
    near_own, near_other = near(rows[:2])
    meta = jnp.concatenate([tags[0]] + [exchange(tags[m], m, 0) for m in (1, 2, 3)] + [pages])
    bias = bias_tiles(rel_bias)
    attn_row = attn_gain.reshape(1, 2 * half)
    final_row = final_gain.reshape(1, 2 * half)
    weights = tuple(
        pltpu.with_memory_space_constraint(w, pltpu.HBM) for w in (w_query, w_key, w_value)
    )
    held = project(0, near_own, near_other, side, attn_row, weights, ())
    queries, keys_local, values_local, packed = project(
        1, far_own, far_other, side, attn_row, weights, tuple(held)
    )
    own_far, send_far = attend(
        (2, 3), meta, segment_ids, side, queries, keys_local, values_local, w_out, bias
    )
    got_far = exchange(send_far, 0, 1)
    own_near, send_near = attend(
        (0, 1), meta, segment_ids, side, queries, keys_local, values_local, w_out, bias
    )
    got_near = exchange(send_near, 0, 1)
    hidden, hidden_two, hidden_three = residual((2, 3), meta, own_far, got_far, packed, ())
    far_first, far_second = far((hidden_two, hidden_three))
    hidden, hidden_zero, hidden_one = residual((0, 1), meta, own_near, got_near, packed, (hidden,))
    near_first, near_second = near((hidden_zero, hidden_one))
    cache = cross(
        (0, 1), meta, side, near_first, near_second, final_row, cross_key, cross_value, ()
    )
    cache = cross(
        (2, 3), meta, side, far_first, far_second, final_row, cross_key, cross_value, (cache,)
    )
    return (hidden.reshape(token_count, half), cache)


def solution(mesh):
    return jax.shard_map(
        shards,
        mesh=mesh,
        in_specs=(
            P("req", "tp"),
            P("req"),
            P("req"),
            P("req"),
            P(),
            P(None, "tp"),
            P(None, "tp"),
            P(None, "tp"),
            P("tp", None),
            P(None, "tp"),
            P(),
            P(None, "tp"),
            P(None, "tp"),
        ),
        out_specs=(P("req", "tp"), P("req", None, None, "tp")),
        check_vma=False,
    )
```

profile of v0, /device:TPU:1, one launch (start us, length us, event | category | flops | bytes accessed | tf_op | source)
XLA Modules:
  0.0 110.0 jit_solution(17060625657803675772)
XLA Ops:
  0.7 1.2 %copy-done.4 = bf16[512,1024]{1,0:T(8,128)(2,1)S(1)} copy-done((bf16[512,1024]{1,0:T(8,128)(2,1)S(1)}, bf16[512,1024]{1,0:T(8,128)(2,1)}, u32[]{:S(2)}) %copy-start.4) | copy-done | bytes 1048600
  1.9 0.7 copy-done.9
  2.5 0.7 copy-done.10
  3.2 1.3 %lane_order.1 = (bf16[128,1024]{1,0:T(8,128)(2,1)S(1)}, bf16[128,1024]{1,0:T(8,128)(2,1)S(1)}, bf16[128,1024]{1,0:T(8,128)(2,1)S(1)}, bf16[128,1024]{1,0:T(8,128...) custom-call(s32[4]{0:T(128)S(1)} %copy-done.9, s32[4]{0:T(128)S(1)} %copy-done.10, ...), custom_call_target="tpu_custom_call" | custom-call | tf_op jit(solution)/shard_map/lane_order/pallas_call | solution.py:77
  4.5 1.5 %collective-permute-start = (s32[2]{0:T(128)S(1)}, s32[2]{0:T(128)S(1)}, u32[]{:S(2)}, u32[]{:S(2)}) collective-permute-start(s32[2]{0:T(128)S(1)} %get-tuple-element.30), channel_id=1, source_target_pairs={{0,2},{1,3},{2,0},{3,1},{4,6},{5,7},{6,4},{7,5},{8,10},{9,11},{10,... | collective-permute-start | bytes 32 | tf_op jit(solution)/shard_map/ppermute | solution.py:23
  6.0 2.8 %collective-permute-start.1 = (s32[2]{0:T(128)S(1)}, s32[2]{0:T(128)S(1)}, u32[]{:S(2)}, u32[]{:S(2)}) collective-permute-start(s32[2]{0:T(128)S(1)} %get-tuple-element.31), channel_id=1, source_target_pairs={{0,4},{1,5},{2,6},{3,7},{4,0},{5,1},{6,2},{7,3},{8,12},{9,13},{10,... | collective-permute-start | bytes 32 | tf_op jit(solution)/shard_map/ppermute | solution.py:23
  8.8 0.4 collective-permute-start.2
  9.2 2.6 %collective-permute-start.3 = (bf16[128,1024]{1,0:T(8,128)(2,1)S(1)}, bf16[128,1024]{1,0:T(8,128)(2,1)S(1)}, u32[]{:S(2)}, u32[]{:S(2)}) collective-permute-start(bf16[128,1024]{1,0:T(8,128)(2,1)S(1)} %get-tuple-element.34), channel_id=1, source_target_pairs={{0,5},{1,4},{2,7},{3,6},{4,1},{5,0},{6,3},{7,2},{8,13},{9,12},{10,... | collective-permute-start | bytes 786440 | tf_op jit(solution)/shard_map/ppermute | solution.py:23
  11.8 0.4 collective-permute-start.5
  12.2 0.1 collective-permute-start.7
  12.3 0.1 collective-permute-start.8
  12.4 0.9 collective-permute-done.2
  13.3 1.1 collective-permute-start.9
  14.4 0.7 copy-done.8
  15.1 1.8 %bias_tiles.1.bias_ref = f32[2048,640]{1,0:T(8,128)S(1)} custom-call(f32[16,32]{1,0:T(8,128)S(1)} %bitcast.17), custom_call_target="tpu_custom_call" | custom-call | bytes 50331648 | tf_op jit(solution)/shard_map/bias_tiles/pallas_call | solution.py:110
  16.9 2.3 %copy-done = f32[2048,640]{1,0:T(8,128)} copy-done((f32[2048,640]{1,0:T(8,128)}, f32[2048,640]{1,0:T(8,128)S(1)}, u32[]{:S(2)}) %copy-start) | copy-done | bytes 5242904
  19.3 0.1 concatenate.3.meta_ref
  19.3 0.0 collective-permute-done.3.s0
  19.3 0.7 collective-permute-start.4
  20.0 4.1 %collective-permute-done.5.s1 = bf16[128,1024]{1,0:T(8,128)(2,1)S(1)} collective-permute-done((bf16[128,1024]{1,0:T(8,128)(2,1)S(1)}, bf16[128,1024]{1,0:T(8,128)(2,1)S(1)}, u32[]{:S(2)}, u32[]{:S(2)}) %collective-permute-start.5) | collective-permute-done | bytes 262176 | tf_op jit(solution)/shard_map/ppermute | solution.py:23
  24.1 0.4 collective-permute-start.6
  24.5 2.4 %collective-permute-done.9.s1 = bf16[128,1024]{1,0:T(8,128)(2,1)S(1)} collective-permute-done((bf16[128,1024]{1,0:T(8,128)(2,1)S(1)}, bf16[128,1024]{1,0:T(8,128)(2,1)S(1)}, u32[]{:S(2)}, u32[]{:S(2)}) %collective-permute-start.9) | collective-permute-done | bytes 262176 | tf_op jit(solution)/shard_map/ppermute | solution.py:23
  26.8 10.0 %project.2 = (bf16[4,128,1024]{2,1,0:T(8,128)(2,1)S(1)}, bf16[4,128,1024]{2,1,0:T(8,128)(2,1)S(1)}, bf16[4,128,1024]{2,1,0:T(8,128)(2,1)S(1)}, bf16[4,128,1024]{2,1,0:T(8,128)(2,1)S(1)}) custom-call(s32[1]{0:T(128)} %bitcast.2.side_ref, bf16[128,1024]{1,0:T(8,128)(2,1)S(1)} %get-tuple-element.36.f0, bf16[128,1024]{1,0:T(8,128)(2,1)S(1)} %collective-permute-done.7.f1, ...), custom_call_target="tpu_custom_call" | custom-call | flops 3221225472 | bytes 4194304 | tf_op jit(solution)/shard_map/project/pallas_call | solution.py:163
  36.9 0.0 copy-start.1
  36.9 0.0 copy-start.6
  36.9 10.0 %project.3 = (bf16[4,128,1024]{2,1,0:T(8,128)(2,1)S(1)}, bf16[4,128,1024]{2,1,0:T(8,128)(2,1)S(1)}, bf16[4,128,1024]{2,1,0:T(8,128)(2,1)S(1)}, bf16[4,128,1024]{2,1,0:T(8,128)(2,1)S(1)}) custom-call(s32[1]{0:T(128)} %bitcast.2.side_ref, ...), custom_call_target="tpu_custom_call", output_to_operand_aliasing={{0}: (9, {}), {1}: (10, {}), {2}: (11, {}), {3}: (12, {})} | custom-call | flops 3221225472 | bytes 4194304 | tf_op jit(solution)/shard_map/project/pallas_call | solution.py:163
  47.0 4.9 %attend.3 = (bf16[256,1024]{1,0:T(8,128)(2,1)S(1)}, bf16[256,1024]{1,0:T(8,128)(2,1)S(1)}) custom-call(s32[12]{0:T(128)S(1)} %concatenate.3.meta_ref, s32[512]{0:T(512)S(1)} %copy-done.6, s32[1]{0:T(128)} %bitcast.2.side_ref, bf16[4,128,1024]{2,1,0:T(8,128)(2,1)S(1)} %get-tuple-element.42.q_ref, bf16[4,128,1024]{2,1,0:T(8,128)(2,1)S(1)} %get-tuple-element.43.k_ref, ...), custom_call_target="tpu_custom_call" | custom-call | flops 2147483648 | bytes 10485760 | tf_op jit(solution)/shard_map/attend/pallas_call | solution.py:289
  51.9 0.2 collective-permute-start.11
  52.0 4.6 %attend.2 = (bf16[256,1024]{1,0:T(8,128)(2,1)S(1)}, bf16[256,1024]{1,0:T(8,128)(2,1)S(1)}) custom-call(s32[12]{0:T(128)S(1)} %concatenate.3.meta_ref, s32[512]{0:T(512)S(1)} %copy-done.6, s32[1]{0:T(128)} %bitcast.2.side_ref, bf16[4,128,1024]{2,1,0:T(8,128)(2,1)S(1)} %get-tuple-element.42.q_ref, bf16[4,128,1024]{2,1,0:T(8,128)(2,1)S(1)} %get-tuple-element.43.k_ref, ...), custom_call_target="tpu_custom_call" | custom-call | flops 2147483648 | bytes 10485760 | tf_op jit(solution)/shard_map/attend/pallas_call | solution.py:289
  56.7 0.0 copy-start.2
  56.7 0.0 copy-start.7
  56.7 1.5 %collective-permute-start.10 = (bf16[256,1024]{1,0:T(8,128)(2,1)S(1)}, bf16[256,1024]{1,0:T(8,128)(2,1)S(1)}, u32[]{:S(2)}, u32[]{:S(2)}) collective-permute-start(bf16[256,1024]{1,0:T(8,128)(2,1)S(1)} %get-tuple-element.46), channel_id=1, source_target_pairs={{0,1},{1,0},{2,3},{3,2},{4,5},{5,4},{6,7},{7,6},{8,9},{9,8},{10,11... | collective-permute-start | bytes 1572872 | tf_op jit(solution)/shard_map/ppermute | solution.py:23
  58.2 6.2 %collective-permute-done.11.got_ref = bf16[256,1024]{1,0:T(8,128)(2,1)S(1)} collective-permute-done((bf16[256,1024]{1,0:T(8,128)(2,1)S(1)}, bf16[256,1024]{1,0:T(8,128)(2,1)S(1)}, u32[]{:S(2)}, u32[]{:S(2)}) %collective-permute-start.11) | collective-permute-done | bytes 524320 | tf_op jit(solution)/shard_map/ppermute | solution.py:23
  64.4 1.5 %residual.2 = (bf16[4,128,1024]{2,1,0:T(8,128)(2,1)}, bf16[128,1024]{1,0:T(8,128)(2,1)S(1)}, bf16[128,1024]{1,0:T(8,128)(2,1)S(1)}) custom-call(s32[12]{0:T(128)S(1)} %concatenate.3.meta_ref, bf16[256,1024]{1,0:T(8,128)(2,1)S(1)} %get-tuple-element.48.own_ref, bf16[256,1024]{1,0:T(8,128)(2,1)S(1)} %collective-permute-done.11.got_ref, ...), custom_call_target="tpu_custom_call" | custom-call | tf_op jit(solution)/shard_map/residual/pallas_call | solution.py:338
  65.9 8.5 %collective-permute-start.14 = (bf16[128,1024]{1,0:T(8,128)(2,1)S(1)}, bf16[128,1024]{1,0:T(8,128)(2,1)S(1)}, u32[]{:S(2)}, u32[]{:S(2)}) collective-permute-start(bf16[128,1024]{1,0:T(8,128)(2,1)S(1)} %get-tuple-element.53), channel_id=1, source_target_pairs={{0,7},{1,6},{2,5},{3,4},{4,3},{5,2},{6,1},{7,0},{8,15},{9,14},{10,... | collective-permute-start | bytes 786440 | tf_op jit(solution)/shard_map/ppermute | solution.py:23
  74.5 1.2 %collective-permute-done.10.got_ref = bf16[256,1024]{1,0:T(8,128)(2,1)S(1)} collective-permute-done((bf16[256,1024]{1,0:T(8,128)(2,1)S(1)}, bf16[256,1024]{1,0:T(8,128)(2,1)S(1)}, u32[]{:S(2)}, u32[]{:S(2)}) %collective-permute-start.10) | collective-permute-done | bytes 524320 | tf_op jit(solution)/shard_map/ppermute | solution.py:23
  75.6 1.5 %residual.3 = (bf16[4,128,1024]{2,1,0:T(8,128)(2,1)}, bf16[128,1024]{1,0:T(8,128)(2,1)S(1)}, bf16[128,1024]{1,0:T(8,128)(2,1)S(1)}) custom-call(s32[12]{0:T(128)S(1)} %concatenate.3.meta_ref, bf16[256,1024]{1,0:T(8,128)(2,1)S(1)} %get-tuple-element.45.own_ref, ...), custom_call_target="tpu_custom_call", output_to_operand_aliasing={{0}: (4, {})} | custom-call | tf_op jit(solution)/shard_map/residual/pallas_call | solution.py:338
  77.2 1.9 %collective-permute-start.16 = (bf16[128,1024]{1,0:T(8,128)(2,1)S(1)}, bf16[128,1024]{1,0:T(8,128)(2,1)S(1)}, u32[]{:S(2)}, u32[]{:S(2)}) collective-permute-start(bf16[128,1024]{1,0:T(8,128)(2,1)S(1)} %get-tuple-element.55), channel_id=1, source_target_pairs={{0,2},{1,3},{2,0},{3,1},{4,6},{5,7},{6,4},{7,5},{8,10},{9,11},{10,... | collective-permute-start | bytes 786440 | tf_op jit(solution)/shard_map/ppermute | solution.py:23
  79.0 0.1 collective-permute-start.17
  79.1 1.6 %collective-permute-start.18 = (bf16[128,1024]{1,0:T(8,128)(2,1)S(1)}, bf16[128,1024]{1,0:T(8,128)(2,1)S(1)}, u32[]{:S(2)}, u32[]{:S(2)}) collective-permute-start(bf16[128,1024]{1,0:T(8,128)(2,1)S(1)} %get-tuple-element.55), channel_id=1, source_target_pairs={{0,3},{1,2},{2,1},{3,0},{4,7},{5,6},{6,5},{7,4},{8,11},{9,10},{10,... | collective-permute-start | bytes 786440 | tf_op jit(solution)/shard_map/ppermute | solution.py:23
  80.7 0.1 collective-permute-start.13
  80.8 3.5 %collective-permute-done.14.s1 = bf16[128,1024]{1,0:T(8,128)(2,1)S(1)} collective-permute-done((bf16[128,1024]{1,0:T(8,128)(2,1)S(1)}, bf16[128,1024]{1,0:T(8,128)(2,1)S(1)}, u32[]{:S(2)}, u32[]{:S(2)}) %collective-permute-start.14) | collective-permute-done | bytes 262176 | tf_op jit(solution)/shard_map/ppermute | solution.py:23
  84.3 0.0 collective-permute-start.15
  84.3 2.7 %collective-permute-done.17.s0 = bf16[128,1024]{1,0:T(8,128)(2,1)S(1)} collective-permute-done((bf16[128,1024]{1,0:T(8,128)(2,1)S(1)}, bf16[128,1024]{1,0:T(8,128)(2,1)S(1)}, u32[]{:S(2)}, u32[]{:S(2)}) %collective-permute-start.17) | collective-permute-done | bytes 262176 | tf_op jit(solution)/shard_map/ppermute | solution.py:23
  87.0 6.1 %collective-permute-done.18.s1 = bf16[128,1024]{1,0:T(8,128)(2,1)S(1)} collective-permute-done((bf16[128,1024]{1,0:T(8,128)(2,1)S(1)}, bf16[128,1024]{1,0:T(8,128)(2,1)S(1)}, u32[]{:S(2)}, u32[]{:S(2)}) %collective-permute-start.18) | collective-permute-done | bytes 262176 | tf_op jit(solution)/shard_map/ppermute | solution.py:23
  93.1 6.0 %cross.2.rest_0_ = bf16[4,128,2,1024]{3,2,1,0:T(2,128)(2,1)} custom-call(s32[12]{0:T(128)S(1)} %concatenate.3.meta_ref, s32[1]{0:T(128)} %bitcast.2.side_ref, bf16[128,1024]{1,0:T(8,128)(2,1)S(1)} %get-tuple-element.54.f0, bf16[128,1024]{1,0:T(8,128)(2,1)S(1)} %collective-permute-done.16.f1, bf16[128,1024]{1,0:T(8,128)(2,1)S(1)} %collective-permute-done.17.s0, ...), custom_call_target="tpu_custom_call" | custom-call | flops 2147483648 | bytes 8388608 | tf_op jit(solution)/shard_map/cross/pallas_call | solution.py:382
  99.1 4.8 %collective-permute-done.15.f1 = bf16[128,1024]{1,0:T(8,128)(2,1)S(1)} collective-permute-done((bf16[128,1024]{1,0:T(8,128)(2,1)S(1)}, bf16[128,1024]{1,0:T(8,128)(2,1)S(1)}, u32[]{:S(2)}, u32[]{:S(2)}) %collective-permute-start.15) | collective-permute-done | bytes 262176 | tf_op jit(solution)/shard_map/ppermute | solution.py:23
  103.8 6.0 %cross.3 = bf16[4,128,2,1024]{3,2,1,0:T(2,128)(2,1)} custom-call(s32[12]{0:T(128)S(1)} %concatenate.3.meta_ref, s32[1]{0:T(128)} %bitcast.2.side_ref, bf16[128,1024]{1,0:T(8,128)(2,1)S(1)} %collective-permute-done.13.f0, bf16[128,1024]{1,0:T(8,128)(2,1)S(1)} %collective-permute-done.15.f1, ...), custom_call_target="tpu_custom_call", output_to_operand_aliasing={{}: (9, {})} | custom-call | flops 2147483648 | bytes 8388608 | tf_op jit(solution)/shard_map/cross/pallas_call | solution.py:382
  (28 shorter events, 0.1 us)
Async XLA Ops:
  0.6 26.2 %copy-start.5 = (f32[2048]{0:T(1024)S(1)}, f32[2048]{0:T(1024)}, u32[]{:S(2)}) copy-start(f32[2048]{0:T(1024)} %param.17) | copy-start | bytes 24580
  0.6 1.2 %copy-start.4 = (bf16[512,1024]{1,0:T(8,128)(2,1)S(1)}, bf16[512,1024]{1,0:T(8,128)(2,1)}, u32[]{:S(2)}) copy-start(bf16[512,1024]{1,0:T(8,128)(2,1)} %param.13) | copy-start | bytes 3145732
  1.9 0.7 copy-start.9
  2.5 0.7 copy-start.10
  4.5 7.7 %collective-permute-start = (s32[2]{0:T(128)S(1)}, s32[2]{0:T(128)S(1)}, u32[]{:S(2)}, u32[]{:S(2)}) collective-permute-start(s32[2]{0:T(128)S(1)} %get-tuple-element.30), channel_id=1, source_target_pairs={{0,2},{1,3},{2,0},{3,1},{4,6},{5,7},{6,4},{7,5},{8,10},{9,11},{10,... | collective-permute-start | bytes 32 | tf_op jit(solution)/shard_map/ppermute | solution.py:23
  6.0 6.3 %collective-permute-start.1 = (s32[2]{0:T(128)S(1)}, s32[2]{0:T(128)S(1)}, u32[]{:S(2)}, u32[]{:S(2)}) collective-permute-start(s32[2]{0:T(128)S(1)} %get-tuple-element.31), channel_id=1, source_target_pairs={{0,4},{1,5},{2,6},{3,7},{4,0},{5,1},{6,2},{7,3},{8,12},{9,13},{10,... | collective-permute-start | bytes 32 | tf_op jit(solution)/shard_map/ppermute | solution.py:23
  8.8 4.5 %collective-permute-start.2 = (s32[2]{0:T(128)S(1)}, s32[2]{0:T(128)S(1)}, u32[]{:S(2)}, u32[]{:S(2)}) collective-permute-start(s32[2]{0:T(128)S(1)} %get-tuple-element.32), channel_id=1, source_target_pairs={{0,6},{1,7},{2,4},{3,5},{4,2},{5,3},{6,0},{7,1},{8,14},{9,15},{10,... | collective-permute-start | bytes 32 | tf_op jit(solution)/shard_map/ppermute | solution.py:23
  9.2 10.1 %collective-permute-start.3 = (bf16[128,1024]{1,0:T(8,128)(2,1)S(1)}, bf16[128,1024]{1,0:T(8,128)(2,1)S(1)}, u32[]{:S(2)}, u32[]{:S(2)}) collective-permute-start(bf16[128,1024]{1,0:T(8,128)(2,1)S(1)} %get-tuple-element.34), channel_id=1, source_target_pairs={{0,5},{1,4},{2,7},{3,6},{4,1},{5,0},{6,3},{7,2},{8,13},{9,12},{10,... | collective-permute-start | bytes 786440 | tf_op jit(solution)/shard_map/ppermute | solution.py:23
  11.8 12.3 %collective-permute-start.5 = (bf16[128,1024]{1,0:T(8,128)(2,1)S(1)}, bf16[128,1024]{1,0:T(8,128)(2,1)S(1)}, u32[]{:S(2)}, u32[]{:S(2)}) collective-permute-start(bf16[128,1024]{1,0:T(8,128)(2,1)S(1)} %get-tuple-element.35), channel_id=1, source_target_pairs={{0,7},{1,6},{2,5},{3,4},{4,3},{5,2},{6,1},{7,0},{8,15},{9,14},{10,... | collective-permute-start | bytes 786440 | tf_op jit(solution)/shard_map/ppermute | solution.py:23
  12.2 12.2 %collective-permute-start.7 = (bf16[128,1024]{1,0:T(8,128)(2,1)S(1)}, bf16[128,1024]{1,0:T(8,128)(2,1)S(1)}, u32[]{:S(2)}, u32[]{:S(2)}) collective-permute-start(bf16[128,1024]{1,0:T(8,128)(2,1)S(1)} %get-tuple-element.37), channel_id=1, source_target_pairs={{0,2},{1,3},{2,0},{3,1},{4,6},{5,7},{6,4},{7,5},{8,10},{9,11},{10,... | collective-permute-start | bytes 786440 | tf_op jit(solution)/shard_map/ppermute | solution.py:23
  12.3 12.2 %collective-permute-start.8 = (bf16[128,1024]{1,0:T(8,128)(2,1)S(1)}, bf16[128,1024]{1,0:T(8,128)(2,1)S(1)}, u32[]{:S(2)}, u32[]{:S(2)}) collective-permute-start(bf16[128,1024]{1,0:T(8,128)(2,1)S(1)} %get-tuple-element.36.f0), channel_id=1, source_target_pairs={{0,1},{1,0},{2,3},{3,2},{4,5},{5,4},{6,7},{7,6},{8,9},{9,8},{10,11... | collective-permute-start | bytes 786440 | tf_op jit(solution)/shard_map/ppermute | solution.py:23
  13.3 13.5 %collective-permute-start.9 = (bf16[128,1024]{1,0:T(8,128)(2,1)S(1)}, bf16[128,1024]{1,0:T(8,128)(2,1)S(1)}, u32[]{:S(2)}, u32[]{:S(2)}) collective-permute-start(bf16[128,1024]{1,0:T(8,128)(2,1)S(1)} %get-tuple-element.37), channel_id=1, source_target_pairs={{0,3},{1,2},{2,1},{3,0},{4,7},{5,6},{6,5},{7,4},{8,11},{9,10},{10,... | collective-permute-start | bytes 786440 | tf_op jit(solution)/shard_map/ppermute | solution.py:23
  14.4 0.7 copy-start.8
  16.9 2.3 %copy-start = (f32[2048,640]{1,0:T(8,128)}, f32[2048,640]{1,0:T(8,128)S(1)}, u32[]{:S(2)}) copy-start(f32[2048,640]{1,0:T(8,128)S(1)} %bias_tiles.1.bias_ref) | copy-start | bytes 15728644
  19.3 17.5 %collective-permute-start.4 = (bf16[128,1024]{1,0:T(8,128)(2,1)S(1)}, bf16[128,1024]{1,0:T(8,128)(2,1)S(1)}, u32[]{:S(2)}, u32[]{:S(2)}) collective-permute-start(bf16[128,1024]{1,0:T(8,128)(2,1)S(1)} %collective-permute-done.3.s0), channel_id=1, source_target_pairs={{0,1},{1,0},{2,3},{3,2},{4,5},{5,4},{6,7},{7,6},{8,9},{9,8},{10,11... | collective-permute-start | bytes 786440 | tf_op jit(solution)/shard_map/ppermute | solution.py:23
  24.1 12.8 %collective-permute-start.6 = (bf16[128,1024]{1,0:T(8,128)(2,1)S(1)}, bf16[128,1024]{1,0:T(8,128)(2,1)S(1)}, u32[]{:S(2)}, u32[]{:S(2)}) collective-permute-start(bf16[128,1024]{1,0:T(8,128)(2,1)S(1)} %collective-permute-done.5.s1), channel_id=1, source_target_pairs={{0,1},{1,0},{2,3},{3,2},{4,5},{5,4},{6,7},{7,6},{8,9},{9,8},{10,11... | collective-permute-start | bytes 786440 | tf_op jit(solution)/shard_map/ppermute | solution.py:23
  26.8 20.1 %slice-start = ((s8[5242880]{0:T(1024)(128)(4,1)}), s8[4194304]{0:T(1024)(128)(4,1)S(1)}, s32[]{:S(2)}) async-start(s8[5242880]{0:T(1024)(128)(4,1)} %bitcast.8), calls=%async_computation | async-start | bytes 8388608
  36.9 10.1 %slice-start.1 = ((s8[5242880]{0:T(1024)(128)(4,1)}), s8[1048576]{0:T(1024)(128)(4,1)S(1)}, s32[]{:S(2)}) async-start(s8[5242880]{0:T(1024)(128)(4,1)} %bitcast.8), calls=%async_computation.1 | async-start | bytes 2097152
  36.9 10.1 %copy-start.1 = (bf16[1024,2048]{1,0:T(8,128)(2,1)S(1)}, bf16[1024,2048]{1,0:T(8,128)(2,1)}, u32[]{:S(2)}) copy-start(bf16[1024,2048]{1,0:T(8,128)(2,1)} %w_ref.3) | copy-start | bytes 12582916
  36.9 10.1 %copy-start.6 = (s32[512]{0:T(512)S(1)}, s32[512]{0:T(512)}, u32[]{:S(2)}) copy-start(s32[512]{0:T(512)} %seg_ref.3) | copy-start | bytes 6148
  51.9 12.5 %collective-permute-start.11 = (bf16[256,1024]{1,0:T(8,128)(2,1)S(1)}, bf16[256,1024]{1,0:T(8,128)(2,1)S(1)}, u32[]{:S(2)}, u32[]{:S(2)}) collective-permute-start(bf16[256,1024]{1,0:T(8,128)(2,1)S(1)} %get-tuple-element.49), channel_id=1, source_target_pairs={{0,1},{1,0},{2,3},{3,2},{4,5},{5,4},{6,7},{7,6},{8,9},{9,8},{10,11... | collective-permute-start | bytes 1572872 | tf_op jit(solution)/shard_map/ppermute | solution.py:23
  52.0 41.0 %copy-start.3 = (bf16[2048,1024]{1,0:T(8,128)(2,1)S(1)}, bf16[2048,1024]{1,0:T(8,128)(2,1)}, u32[]{:S(2)}) copy-start(bf16[2048,1024]{1,0:T(8,128)(2,1)} %wv.7) | copy-start | bytes 12582916
  56.7 36.4 %copy-start.2 = (bf16[2048,1024]{1,0:T(8,128)(2,1)S(1)}, bf16[2048,1024]{1,0:T(8,128)(2,1)}, u32[]{:S(2)}) copy-start(bf16[2048,1024]{1,0:T(8,128)(2,1)} %wk.7) | copy-start | bytes 12582916
  56.7 36.4 %copy-start.7 = (f32[2048]{0:T(1024)S(1)}, f32[2048]{0:T(1024)}, u32[]{:S(2)}) copy-start(f32[2048]{0:T(1024)} %param.23) | copy-start | bytes 24580
  56.7 18.9 %collective-permute-start.10 = (bf16[256,1024]{1,0:T(8,128)(2,1)S(1)}, bf16[256,1024]{1,0:T(8,128)(2,1)S(1)}, u32[]{:S(2)}, u32[]{:S(2)}) collective-permute-start(bf16[256,1024]{1,0:T(8,128)(2,1)S(1)} %get-tuple-element.46), channel_id=1, source_target_pairs={{0,1},{1,0},{2,3},{3,2},{4,5},{5,4},{6,7},{7,6},{8,9},{9,8},{10,11... | collective-permute-start | bytes 1572872 | tf_op jit(solution)/shard_map/ppermute | solution.py:23
  65.9 14.8 %collective-permute-start.12 = (bf16[128,1024]{1,0:T(8,128)(2,1)S(1)}, bf16[128,1024]{1,0:T(8,128)(2,1)S(1)}, u32[]{:S(2)}, u32[]{:S(2)}) collective-permute-start(bf16[128,1024]{1,0:T(8,128)(2,1)S(1)} %get-tuple-element.52), channel_id=1, source_target_pairs={{0,5},{1,4},{2,7},{3,6},{4,1},{5,0},{6,3},{7,2},{8,13},{9,12},{10,... | collective-permute-start | bytes 786440 | tf_op jit(solution)/shard_map/ppermute | solution.py:23
  65.9 18.4 %collective-permute-start.14 = (bf16[128,1024]{1,0:T(8,128)(2,1)S(1)}, bf16[128,1024]{1,0:T(8,128)(2,1)S(1)}, u32[]{:S(2)}, u32[]{:S(2)}) collective-permute-start(bf16[128,1024]{1,0:T(8,128)(2,1)S(1)} %get-tuple-element.53), channel_id=1, source_target_pairs={{0,7},{1,6},{2,5},{3,4},{4,3},{5,2},{6,1},{7,0},{8,15},{9,14},{10,... | collective-permute-start | bytes 786440 | tf_op jit(solution)/shard_map/ppermute | solution.py:23
  77.2 7.1 %collective-permute-start.16 = (bf16[128,1024]{1,0:T(8,128)(2,1)S(1)}, bf16[128,1024]{1,0:T(8,128)(2,1)S(1)}, u32[]{:S(2)}, u32[]{:S(2)}) collective-permute-start(bf16[128,1024]{1,0:T(8,128)(2,1)S(1)} %get-tuple-element.55), channel_id=1, source_target_pairs={{0,2},{1,3},{2,0},{3,1},{4,6},{5,7},{6,4},{7,5},{8,10},{9,11},{10,... | collective-permute-start | bytes 786440 | tf_op jit(solution)/shard_map/ppermute | solution.py:23
  79.0 7.9 %collective-permute-start.17 = (bf16[128,1024]{1,0:T(8,128)(2,1)S(1)}, bf16[128,1024]{1,0:T(8,128)(2,1)S(1)}, u32[]{:S(2)}, u32[]{:S(2)}) collective-permute-start(bf16[128,1024]{1,0:T(8,128)(2,1)S(1)} %get-tuple-element.54.f0), channel_id=1, source_target_pairs={{0,1},{1,0},{2,3},{3,2},{4,5},{5,4},{6,7},{7,6},{8,9},{9,8},{10,11... | collective-permute-start | bytes 786440 | tf_op jit(solution)/shard_map/ppermute | solution.py:23
  79.1 14.0 %collective-permute-start.18 = (bf16[128,1024]{1,0:T(8,128)(2,1)S(1)}, bf16[128,1024]{1,0:T(8,128)(2,1)S(1)}, u32[]{:S(2)}, u32[]{:S(2)}) collective-permute-start(bf16[128,1024]{1,0:T(8,128)(2,1)S(1)} %get-tuple-element.55), channel_id=1, source_target_pairs={{0,3},{1,2},{2,1},{3,0},{4,7},{5,6},{6,5},{7,4},{8,11},{9,10},{10,... | collective-permute-start | bytes 786440 | tf_op jit(solution)/shard_map/ppermute | solution.py:23
  80.7 18.4 %collective-permute-start.13 = (bf16[128,1024]{1,0:T(8,128)(2,1)S(1)}, bf16[128,1024]{1,0:T(8,128)(2,1)S(1)}, u32[]{:S(2)}, u32[]{:S(2)}) collective-permute-start(bf16[128,1024]{1,0:T(8,128)(2,1)S(1)} %collective-permute-done.12.s0), channel_id=1, source_target_pairs={{0,1},{1,0},{2,3},{3,2},{4,5},{5,4},{6,7},{7,6},{8,9},{9,8},{10,11... | collective-permute-start | bytes 786440 | tf_op jit(solution)/shard_map/ppermute | solution.py:23
  84.3 19.5 %collective-permute-start.15 = (bf16[128,1024]{1,0:T(8,128)(2,1)S(1)}, bf16[128,1024]{1,0:T(8,128)(2,1)S(1)}, u32[]{:S(2)}, u32[]{:S(2)}) collective-permute-start(bf16[128,1024]{1,0:T(8,128)(2,1)S(1)} %collective-permute-done.14.s1), channel_id=1, source_target_pairs={{0,1},{1,0},{2,3},{3,2},{4,5},{5,4},{6,7},{7,6},{8,9},{9,8},{10,11... | collective-permute-start | bytes 786440 | tf_op jit(solution)/shard_map/ppermute | solution.py:23
where the time goes:
time: 110 us
  Pallas kernels  47.6 us (43%)
  waiting for transfers between devices  31.9 us (29%)
  starting transfers between devices  23.8 us (22%)
  local copies, waits for them, and re-layouts  5.65 us (5%)
    ppermute x19, waiting for transfers between devices, exchange(): return lax.ppermute(block, ('req', 'tp'), pairs)  31.9 us
    ppermute x19, starting transfers between devices, exchange(): return lax.ppermute(block, ('req', 'tp'), pairs)  23.8 us
    pallas_call x2, Pallas kernels, project(): pl.pallas_call(body, grid_spec=pltpu.PrefetchScalarGridSpec(num_scalar_pr...  20 us
    pallas_call x2, Pallas kernels, cross(): pl.pallas_call(body, grid_spec=pltpu.PrefetchScalarGridSpec(num_scalar_pr...  11.9 us
    pallas_call x2, Pallas kernels, attend(): pl.pallas_call(body, grid_spec=pltpu.PrefetchScalarGridSpec(num_scalar_pr...  9.5 us
    unnamed x26, local copies, waits for them, and re-layouts  5.57 us
    pallas_call x2, Pallas kernels, residual(): pl.pallas_call(body, grid_spec=pltpu.PrefetchScalarGridSpec(num_scalar_pr...  3.03 us
  transfers between devices with their start and end apart: 19, of which 9 were waited for; matrix products, arithmetic and copies ran while one was open for 0% of the time, Pallas kernels for 23%

commit v1 on v0

--- a/solution.py
+++ b/solution.py
@@ -141,19 +141,17 @@
     def body(side_ref, f0, f1, s0, s1, gain_ref, wq, wk, wv, *rest):
         q_out, k_out, v_out, own_out, normed, held, sems = rest[-7:]
         copies = []
-        for n, start in enumerate(starts):
-            here = slice(start, start + GROUP)
-            for i, w_ref in enumerate((wq, wk, wv)):
-                copy = pltpu.make_async_copy(w_ref.at[:, here], held.at[i, :, here], sems.at[n, i])
-                copy.start()
-                copies.append(copy)
+        for i, w_ref in enumerate((wq, wk, wv)):
+            copy = pltpu.make_async_copy(w_ref, held.at[i], sems.at[i])
+            copy.start()
+            copies.append(copy)
         normalize(side_ref[0], (f0, f1), (s0, s1), gain_ref, normed)
         own_out[0] = f0[...]
         own_out[1] = f1[...]
-        for n, start in enumerate(starts):
-            here = slice(start, start + GROUP)
-            for i, out in enumerate((q_out, k_out, v_out)):
-                copies[3 * n + i].wait()
+        for i, out in enumerate((q_out, k_out, v_out)):
+            copies[i].wait()
+            for start in starts:
+                here = slice(start, start + GROUP)
                 product = jnp.dot(normed[...], held[i, :, here], preferred_element_type=jnp.float32)
                 out[:, :, here] = product.astype(jnp.bfloat16).reshape(2, PAGE, GROUP)
 
@@ -170,7 +168,7 @@
             scratch_shapes=[
                 pltpu.VMEM((2 * PAGE, 2 * half), jnp.bfloat16),
                 pltpu.VMEM((3, 2 * half, columns), jnp.bfloat16),
-                pltpu.SemaphoreType.DMA((len(starts), 3)),
+                pltpu.SemaphoreType.DMA((3,)),
             ],
         ),
         out_shape=[shape, shape, shape, jax.ShapeDtypeStruct((4, PAGE, half), jnp.bfloat16)],

time: 110 us -> 107 us (0.973)
  waiting for transfers between devices: 31.9 us -> 39.9 us
  starting transfers between devices: 23.8 us -> 18.3 us
  Pallas kernels: 47.6 us -> 42.3 us
    ppermute x19, waiting for transfers between devices: 31.9 us -> 39.9 us  [exchange(): return lax.ppermute(block, ('req', 'tp'), pairs)]
    pallas_call x2, Pallas kernels: 20 us -> 12.3 us  [project(): pl.pallas_call(body, grid_spec=pltpu.PrefetchScalarGridSpec(num_scalar_pr...]
    ppermute x19, starting transfers between devices: 23.8 us -> 18.3 us  [exchange(): return lax.ppermute(block, ('req', 'tp'), pairs)]
    pallas_call x2, Pallas kernels: 9.5 us -> 12 us  [attend(): pl.pallas_call(body, grid_spec=pltpu.PrefetchScalarGridSpec(num_scalar_pr...]
  transfers between devices with their start and end apart: 19 -> 19, of which waited for: 9 -> 10; matrix products, arithmetic and copies ran while one was open for 0% -> 0% of each run, Pallas kernels for 23% -> 21%
where the time goes in v1:
time: 107 us
  Pallas kernels  42.3 us (40%)
  waiting for transfers between devices  39.9 us (37%)
  starting transfers between devices  18.3 us (17%)
  local copies, waits for them, and re-layouts  5.64 us (5%)
    ppermute x19, waiting for transfers between devices, exchange(): return lax.ppermute(block, ('req', 'tp'), pairs)  39.9 us
    ppermute x19, starting transfers between devices, exchange(): return lax.ppermute(block, ('req', 'tp'), pairs)  18.3 us
    pallas_call x2, Pallas kernels, project(): pl.pallas_call(body, grid_spec=pltpu.PrefetchScalarGridSpec(num_scalar_pr...  12.3 us
    pallas_call x2, Pallas kernels, attend(): pl.pallas_call(body, grid_spec=pltpu.PrefetchScalarGridSpec(num_scalar_pr...  12 us
    pallas_call x2, Pallas kernels, cross(): pl.pallas_call(body, grid_spec=pltpu.PrefetchScalarGridSpec(num_scalar_pr...  11.9 us
    unnamed x26, local copies, waits for them, and re-layouts  5.57 us
    pallas_call x2, Pallas kernels, residual(): pl.pallas_call(body, grid_spec=pltpu.PrefetchScalarGridSpec(num_scalar_pr...  3.03 us
  transfers between devices with their start and end apart: 19, of which 10 were waited for; matrix products, arithmetic and copies ran while one was open for 0% of the time, Pallas kernels for 21%

profile of v1, /device:TPU:1, one launch (start us, length us, event | category | flops | bytes accessed | tf_op | source)
XLA Modules:
  0.0 107.1 jit_solution(15757472545196239716)
XLA Ops:
  0.7 1.2 %copy-done.4 = bf16[512,1024]{1,0:T(8,128)(2,1)S(1)} copy-done((bf16[512,1024]{1,0:T(8,128)(2,1)S(1)}, bf16[512,1024]{1,0:T(8,128)(2,1)}, u32[]{:S(2)}) %copy-start.4) | copy-done | bytes 1048600
  1.9 0.7 copy-done.9
  2.5 0.7 copy-done.10
  3.2 1.3 %lane_order.1 = (bf16[128,1024]{1,0:T(8,128)(2,1)S(1)}, bf16[128,1024]{1,0:T(8,128)(2,1)S(1)}, bf16[128,1024]{1,0:T(8,128)(2,1)S(1)}, bf16[128,1024]{1,0:T(8,128...) custom-call(s32[4]{0:T(128)S(1)} %copy-done.9, s32[4]{0:T(128)S(1)} %copy-done.10, ...), custom_call_target="tpu_custom_call" | custom-call | tf_op jit(solution)/shard_map/lane_order/pallas_call | solution.py:77
  4.5 1.5 %collective-permute-start = (s32[2]{0:T(128)S(1)}, s32[2]{0:T(128)S(1)}, u32[]{:S(2)}, u32[]{:S(2)}) collective-permute-start(s32[2]{0:T(128)S(1)} %get-tuple-element.30), channel_id=1, source_target_pairs={{0,2},{1,3},{2,0},{3,1},{4,6},{5,7},{6,4},{7,5},{8,10},{9,11},{10,... | collective-permute-start | bytes 32 | tf_op jit(solution)/shard_map/ppermute | solution.py:23
  6.0 2.8 %collective-permute-start.1 = (s32[2]{0:T(128)S(1)}, s32[2]{0:T(128)S(1)}, u32[]{:S(2)}, u32[]{:S(2)}) collective-permute-start(s32[2]{0:T(128)S(1)} %get-tuple-element.31), channel_id=1, source_target_pairs={{0,4},{1,5},{2,6},{3,7},{4,0},{5,1},{6,2},{7,3},{8,12},{9,13},{10,... | collective-permute-start | bytes 32 | tf_op jit(solution)/shard_map/ppermute | solution.py:23
  8.8 0.4 collective-permute-start.2
  9.2 2.6 %collective-permute-start.3 = (bf16[128,1024]{1,0:T(8,128)(2,1)S(1)}, bf16[128,1024]{1,0:T(8,128)(2,1)S(1)}, u32[]{:S(2)}, u32[]{:S(2)}) collective-permute-start(bf16[128,1024]{1,0:T(8,128)(2,1)S(1)} %get-tuple-element.34), channel_id=1, source_target_pairs={{0,5},{1,4},{2,7},{3,6},{4,1},{5,0},{6,3},{7,2},{8,13},{9,12},{10,... | collective-permute-start | bytes 786440 | tf_op jit(solution)/shard_map/ppermute | solution.py:23
  11.8 0.4 collective-permute-start.5
  12.2 0.1 collective-permute-start.7
  12.3 0.1 collective-permute-start.8
  12.4 0.9 collective-permute-done.2
  13.3 1.1 %collective-permute-start.9 = (bf16[128,1024]{1,0:T(8,128)(2,1)S(1)}, bf16[128,1024]{1,0:T(8,128)(2,1)S(1)}, u32[]{:S(2)}, u32[]{:S(2)}) collective-permute-start(bf16[128,1024]{1,0:T(8,128)(2,1)S(1)} %get-tuple-element.37), channel_id=1, source_target_pairs={{0,3},{1,2},{2,1},{3,0},{4,7},{5,6},{6,5},{7,4},{8,11},{9,10},{10,... | collective-permute-start | bytes 786440 | tf_op jit(solution)/shard_map/ppermute | solution.py:23
  14.4 0.7 copy-done.8
  15.1 1.8 %bias_tiles.1.bias_ref = f32[2048,640]{1,0:T(8,128)S(1)} custom-call(f32[16,32]{1,0:T(8,128)S(1)} %bitcast.17), custom_call_target="tpu_custom_call" | custom-call | bytes 50331648 | tf_op jit(solution)/shard_map/bias_tiles/pallas_call | solution.py:110
  16.9 2.3 %copy-done = f32[2048,640]{1,0:T(8,128)} copy-done((f32[2048,640]{1,0:T(8,128)}, f32[2048,640]{1,0:T(8,128)S(1)}, u32[]{:S(2)}) %copy-start) | copy-done | bytes 5242904
  19.3 0.1 concatenate.3.meta_ref
  19.3 0.0 collective-permute-done.3.s0
  19.3 0.7 collective-permute-start.4
  20.0 4.1 %collective-permute-done.5.s1 = bf16[128,1024]{1,0:T(8,128)(2,1)S(1)} collective-permute-done((bf16[128,1024]{1,0:T(8,128)(2,1)S(1)}, bf16[128,1024]{1,0:T(8,128)(2,1)S(1)}, u32[]{:S(2)}, u32[]{:S(2)}) %collective-permute-start.5) | collective-permute-done | bytes 262176 | tf_op jit(solution)/shard_map/ppermute | solution.py:23
  24.1 0.4 collective-permute-start.6
  24.5 2.4 %collective-permute-done.9.s1 = bf16[128,1024]{1,0:T(8,128)(2,1)S(1)} collective-permute-done((bf16[128,1024]{1,0:T(8,128)(2,1)S(1)}, bf16[128,1024]{1,0:T(8,128)(2,1)S(1)}, u32[]{:S(2)}, u32[]{:S(2)}) %collective-permute-start.9) | collective-permute-done | bytes 262176 | tf_op jit(solution)/shard_map/ppermute | solution.py:23
  26.8 6.1 %project.2 = (bf16[4,128,1024]{2,1,0:T(8,128)(2,1)S(1)}, bf16[4,128,1024]{2,1,0:T(8,128)(2,1)S(1)}, bf16[4,128,1024]{2,1,0:T(8,128)(2,1)S(1)}, bf16[4,128,1024]{2,1,0:T(8,128)(2,1)S(1)}) custom-call(s32[1]{0:T(128)} %bitcast.2.side_ref, bf16[128,1024]{1,0:T(8,128)(2,1)S(1)} %get-tuple-element.36.f0, bf16[128,1024]{1,0:T(8,128)(2,1)S(1)} %collective-permute-done.7.f1, ...), custom_call_target="tpu_custom_call" | custom-call | flops 3221225472 | bytes 4194304 | tf_op jit(solution)/shard_map/project/pallas_call | solution.py:161
  33.0 0.0 collective-permute-done.4.f0
  33.0 3.6 %collective-permute-done.6.f1 = bf16[128,1024]{1,0:T(8,128)(2,1)S(1)} collective-permute-done((bf16[128,1024]{1,0:T(8,128)(2,1)S(1)}, bf16[128,1024]{1,0:T(8,128)(2,1)S(1)}, u32[]{:S(2)}, u32[]{:S(2)}) %collective-permute-start.6) | collective-permute-done | bytes 262176 | tf_op jit(solution)/shard_map/ppermute | solution.py:23
  36.6 6.1 %project.3 = (bf16[4,128,1024]{2,1,0:T(8,128)(2,1)S(1)}, bf16[4,128,1024]{2,1,0:T(8,128)(2,1)S(1)}, bf16[4,128,1024]{2,1,0:T(8,128)(2,1)S(1)}, bf16[4,128,1024]{2,1,0:T(8,128)(2,1)S(1)}) custom-call(s32[1]{0:T(128)} %bitcast.2.side_ref, ...), custom_call_target="tpu_custom_call", output_to_operand_aliasing={{0}: (9, {}), {1}: (10, {}), {2}: (11, {}), {3}: (12, {})} | custom-call | flops 3221225472 | bytes 4194304 | tf_op jit(solution)/shard_map/project/pallas_call | solution.py:161
  42.8 6.0 %attend.3 = (bf16[256,1024]{1,0:T(8,128)(2,1)S(1)}, bf16[256,1024]{1,0:T(8,128)(2,1)S(1)}) custom-call(s32[12]{0:T(128)S(1)} %concatenate.3.meta_ref, s32[512]{0:T(512)S(1)} %copy-done.6, s32[1]{0:T(128)} %bitcast.2.side_ref, bf16[4,128,1024]{2,1,0:T(8,128)(2,1)S(1)} %get-tuple-element.42.q_ref, bf16[4,128,1024]{2,1,0:T(8,128)(2,1)S(1)} %get-tuple-element.43.k_ref, ...), custom_call_target="tpu_custom_call" | custom-call | flops 2147483648 | bytes 10485760 | tf_op jit(solution)/shard_map/attend/pallas_call | solution.py:287
  48.8 0.4 collective-permute-start.11
  49.2 6.0 %attend.2 = (bf16[256,1024]{1,0:T(8,128)(2,1)S(1)}, bf16[256,1024]{1,0:T(8,128)(2,1)S(1)}) custom-call(s32[12]{0:T(128)S(1)} %concatenate.3.meta_ref, s32[512]{0:T(512)S(1)} %copy-done.6, s32[1]{0:T(128)} %bitcast.2.side_ref, bf16[4,128,1024]{2,1,0:T(8,128)(2,1)S(1)} %get-tuple-element.42.q_ref, bf16[4,128,1024]{2,1,0:T(8,128)(2,1)S(1)} %get-tuple-element.43.k_ref, ...), custom_call_target="tpu_custom_call" | custom-call | flops 2147483648 | bytes 10485760 | tf_op jit(solution)/shard_map/attend/pallas_call | solution.py:287
  55.2 0.0 copy-start.2
  55.2 0.0 copy-start.7
  55.2 1.5 %collective-permute-start.10 = (bf16[256,1024]{1,0:T(8,128)(2,1)S(1)}, bf16[256,1024]{1,0:T(8,128)(2,1)S(1)}, u32[]{:S(2)}, u32[]{:S(2)}) collective-permute-start(bf16[256,1024]{1,0:T(8,128)(2,1)S(1)} %get-tuple-element.46), channel_id=1, source_target_pairs={{0,1},{1,0},{2,3},{3,2},{4,5},{5,4},{6,7},{7,6},{8,9},{9,8},{10,11... | collective-permute-start | bytes 1572872 | tf_op jit(solution)/shard_map/ppermute | solution.py:23
  56.7 6.1 %collective-permute-done.11.got_ref = bf16[256,1024]{1,0:T(8,128)(2,1)S(1)} collective-permute-done((bf16[256,1024]{1,0:T(8,128)(2,1)S(1)}, bf16[256,1024]{1,0:T(8,128)(2,1)S(1)}, u32[]{:S(2)}, u32[]{:S(2)}) %collective-permute-start.11) | collective-permute-done | bytes 524320 | tf_op jit(solution)/shard_map/ppermute | solution.py:23
  62.7 1.5 %residual.2 = (bf16[4,128,1024]{2,1,0:T(8,128)(2,1)}, bf16[128,1024]{1,0:T(8,128)(2,1)S(1)}, bf16[128,1024]{1,0:T(8,128)(2,1)S(1)}) custom-call(s32[12]{0:T(128)S(1)} %concatenate.3.meta_ref, bf16[256,1024]{1,0:T(8,128)(2,1)S(1)} %get-tuple-element.48.own_ref, bf16[256,1024]{1,0:T(8,128)(2,1)S(1)} %collective-permute-done.11.got_ref, ...), custom_call_target="tpu_custom_call" | custom-call | tf_op jit(solution)/shard_map/residual/pallas_call | solution.py:336
  64.3 3.8 %collective-permute-start.14 = (bf16[128,1024]{1,0:T(8,128)(2,1)S(1)}, bf16[128,1024]{1,0:T(8,128)(2,1)S(1)}, u32[]{:S(2)}, u32[]{:S(2)}) collective-permute-start(bf16[128,1024]{1,0:T(8,128)(2,1)S(1)} %get-tuple-element.53), channel_id=1, source_target_pairs={{0,7},{1,6},{2,5},{3,4},{4,3},{5,2},{6,1},{7,0},{8,15},{9,14},{10,... | collective-permute-start | bytes 786440 | tf_op jit(solution)/shard_map/ppermute | solution.py:23
  68.1 5.9 %collective-permute-done.10.got_ref = bf16[256,1024]{1,0:T(8,128)(2,1)S(1)} collective-permute-done((bf16[256,1024]{1,0:T(8,128)(2,1)S(1)}, bf16[256,1024]{1,0:T(8,128)(2,1)S(1)}, u32[]{:S(2)}, u32[]{:S(2)}) %collective-permute-start.10) | collective-permute-done | bytes 524320 | tf_op jit(solution)/shard_map/ppermute | solution.py:23
  74.0 1.5 %residual.3 = (bf16[4,128,1024]{2,1,0:T(8,128)(2,1)}, bf16[128,1024]{1,0:T(8,128)(2,1)S(1)}, bf16[128,1024]{1,0:T(8,128)(2,1)S(1)}) custom-call(s32[12]{0:T(128)S(1)} %concatenate.3.meta_ref, bf16[256,1024]{1,0:T(8,128)(2,1)S(1)} %get-tuple-element.45.own_ref, ...), custom_call_target="tpu_custom_call", output_to_operand_aliasing={{0}: (4, {})} | custom-call | tf_op jit(solution)/shard_map/residual/pallas_call | solution.py:336
  75.5 0.7 collective-permute-start.16
  76.2 0.1 collective-permute-start.17
  76.3 1.6 %collective-permute-start.18 = (bf16[128,1024]{1,0:T(8,128)(2,1)S(1)}, bf16[128,1024]{1,0:T(8,128)(2,1)S(1)}, u32[]{:S(2)}, u32[]{:S(2)}) collective-permute-start(bf16[128,1024]{1,0:T(8,128)(2,1)S(1)} %get-tuple-element.55), channel_id=1, source_target_pairs={{0,3},{1,2},{2,1},{3,0},{4,7},{5,6},{6,5},{7,4},{8,11},{9,10},{10,... | collective-permute-start | bytes 786440 | tf_op jit(solution)/shard_map/ppermute | solution.py:23
  77.8 0.1 collective-permute-start.13
  77.9 1.2 %collective-permute-done.14.s1 = bf16[128,1024]{1,0:T(8,128)(2,1)S(1)} collective-permute-done((bf16[128,1024]{1,0:T(8,128)(2,1)S(1)}, bf16[128,1024]{1,0:T(8,128)(2,1)S(1)}, u32[]{:S(2)}, u32[]{:S(2)}) %collective-permute-start.14) | collective-permute-done | bytes 262176 | tf_op jit(solution)/shard_map/ppermute | solution.py:23
  79.1 0.2 collective-permute-start.15
  79.3 4.8 %collective-permute-done.17.s0 = bf16[128,1024]{1,0:T(8,128)(2,1)S(1)} collective-permute-done((bf16[128,1024]{1,0:T(8,128)(2,1)S(1)}, bf16[128,1024]{1,0:T(8,128)(2,1)S(1)}, u32[]{:S(2)}, u32[]{:S(2)}) %collective-permute-start.17) | collective-permute-done | bytes 262176 | tf_op jit(solution)/shard_map/ppermute | solution.py:23
  84.1 6.1 %collective-permute-done.18.s1 = bf16[128,1024]{1,0:T(8,128)(2,1)S(1)} collective-permute-done((bf16[128,1024]{1,0:T(8,128)(2,1)S(1)}, bf16[128,1024]{1,0:T(8,128)(2,1)S(1)}, u32[]{:S(2)}, u32[]{:S(2)}) %collective-permute-start.18) | collective-permute-done | bytes 262176 | tf_op jit(solution)/shard_map/ppermute | solution.py:23
  90.2 6.0 %cross.2.rest_0_ = bf16[4,128,2,1024]{3,2,1,0:T(2,128)(2,1)} custom-call(s32[12]{0:T(128)S(1)} %concatenate.3.meta_ref, s32[1]{0:T(128)} %bitcast.2.side_ref, bf16[128,1024]{1,0:T(8,128)(2,1)S(1)} %get-tuple-element.54.f0, bf16[128,1024]{1,0:T(8,128)(2,1)S(1)} %collective-permute-done.16.f1, bf16[128,1024]{1,0:T(8,128)(2,1)S(1)} %collective-permute-done.17.s0, ...), custom_call_target="tpu_custom_call" | custom-call | flops 2147483648 | bytes 8388608 | tf_op jit(solution)/shard_map/cross/pallas_call | solution.py:380
  96.2 4.8 %collective-permute-done.15.f1 = bf16[128,1024]{1,0:T(8,128)(2,1)S(1)} collective-permute-done((bf16[128,1024]{1,0:T(8,128)(2,1)S(1)}, bf16[128,1024]{1,0:T(8,128)(2,1)S(1)}, u32[]{:S(2)}, u32[]{:S(2)}) %collective-permute-start.15) | collective-permute-done | bytes 262176 | tf_op jit(solution)/shard_map/ppermute | solution.py:23
  101.0 6.0 %cross.3 = bf16[4,128,2,1024]{3,2,1,0:T(2,128)(2,1)} custom-call(s32[12]{0:T(128)S(1)} %concatenate.3.meta_ref, s32[1]{0:T(128)} %bitcast.2.side_ref, bf16[128,1024]{1,0:T(8,128)(2,1)S(1)} %collective-permute-done.13.f0, bf16[128,1024]{1,0:T(8,128)(2,1)S(1)} %collective-permute-done.15.f1, ...), custom_call_target="tpu_custom_call", output_to_operand_aliasing={{}: (9, {})} | custom-call | flops 2147483648 | bytes 8388608 | tf_op jit(solution)/shard_map/cross/pallas_call | solution.py:380
  (28 shorter events, 0.1 us)
Async XLA Ops:
  0.6 26.2 %copy-start.5 = (f32[2048]{0:T(1024)S(1)}, f32[2048]{0:T(1024)}, u32[]{:S(2)}) copy-start(f32[2048]{0:T(1024)} %param.17) | copy-start | bytes 24580
  0.6 1.2 %copy-start.4 = (bf16[512,1024]{1,0:T(8,128)(2,1)S(1)}, bf16[512,1024]{1,0:T(8,128)(2,1)}, u32[]{:S(2)}) copy-start(bf16[512,1024]{1,0:T(8,128)(2,1)} %param.13) | copy-start | bytes 3145732
  1.9 0.7 copy-start.9
  2.5 0.7 copy-start.10
  4.5 7.7 %collective-permute-start = (s32[2]{0:T(128)S(1)}, s32[2]{0:T(128)S(1)}, u32[]{:S(2)}, u32[]{:S(2)}) collective-permute-start(s32[2]{0:T(128)S(1)} %get-tuple-element.30), channel_id=1, source_target_pairs={{0,2},{1,3},{2,0},{3,1},{4,6},{5,7},{6,4},{7,5},{8,10},{9,11},{10,... | collective-permute-start | bytes 32 | tf_op jit(solution)/shard_map/ppermute | solution.py:23
  6.0 6.3 %collective-permute-start.1 = (s32[2]{0:T(128)S(1)}, s32[2]{0:T(128)S(1)}, u32[]{:S(2)}, u32[]{:S(2)}) collective-permute-start(s32[2]{0:T(128)S(1)} %get-tuple-element.31), channel_id=1, source_target_pairs={{0,4},{1,5},{2,6},{3,7},{4,0},{5,1},{6,2},{7,3},{8,12},{9,13},{10,... | collective-permute-start | bytes 32 | tf_op jit(solution)/shard_map/ppermute | solution.py:23
  8.8 4.5 %collective-permute-start.2 = (s32[2]{0:T(128)S(1)}, s32[2]{0:T(128)S(1)}, u32[]{:S(2)}, u32[]{:S(2)}) collective-permute-start(s32[2]{0:T(128)S(1)} %get-tuple-element.32), channel_id=1, source_target_pairs={{0,6},{1,7},{2,4},{3,5},{4,2},{5,3},{6,0},{7,1},{8,14},{9,15},{10,... | collective-permute-start | bytes 32 | tf_op jit(solution)/shard_map/ppermute | solution.py:23
  9.2 10.1 %collective-permute-start.3 = (bf16[128,1024]{1,0:T(8,128)(2,1)S(1)}, bf16[128,1024]{1,0:T(8,128)(2,1)S(1)}, u32[]{:S(2)}, u32[]{:S(2)}) collective-permute-start(bf16[128,1024]{1,0:T(8,128)(2,1)S(1)} %get-tuple-element.34), channel_id=1, source_target_pairs={{0,5},{1,4},{2,7},{3,6},{4,1},{5,0},{6,3},{7,2},{8,13},{9,12},{10,... | collective-permute-start | bytes 786440 | tf_op jit(solution)/shard_map/ppermute | solution.py:23
  11.8 12.3 %collective-permute-start.5 = (bf16[128,1024]{1,0:T(8,128)(2,1)S(1)}, bf16[128,1024]{1,0:T(8,128)(2,1)S(1)}, u32[]{:S(2)}, u32[]{:S(2)}) collective-permute-start(bf16[128,1024]{1,0:T(8,128)(2,1)S(1)} %get-tuple-element.35), channel_id=1, source_target_pairs={{0,7},{1,6},{2,5},{3,4},{4,3},{5,2},{6,1},{7,0},{8,15},{9,14},{10,... | collective-permute-start | bytes 786440 | tf_op jit(solution)/shard_map/ppermute | solution.py:23
  12.2 12.2 %collective-permute-start.7 = (bf16[128,1024]{1,0:T(8,128)(2,1)S(1)}, bf16[128,1024]{1,0:T(8,128)(2,1)S(1)}, u32[]{:S(2)}, u32[]{:S(2)}) collective-permute-start(bf16[128,1024]{1,0:T(8,128)(2,1)S(1)} %get-tuple-element.37), channel_id=1, source_target_pairs={{0,2},{1,3},{2,0},{3,1},{4,6},{5,7},{6,4},{7,5},{8,10},{9,11},{10,... | collective-permute-start | bytes 786440 | tf_op jit(solution)/shard_map/ppermute | solution.py:23
  12.3 12.2 %collective-permute-start.8 = (bf16[128,1024]{1,0:T(8,128)(2,1)S(1)}, bf16[128,1024]{1,0:T(8,128)(2,1)S(1)}, u32[]{:S(2)}, u32[]{:S(2)}) collective-permute-start(bf16[128,1024]{1,0:T(8,128)(2,1)S(1)} %get-tuple-element.36.f0), channel_id=1, source_target_pairs={{0,1},{1,0},{2,3},{3,2},{4,5},{5,4},{6,7},{7,6},{8,9},{9,8},{10,11... | collective-permute-start | bytes 786440 | tf_op jit(solution)/shard_map/ppermute | solution.py:23
  13.3 13.5 %collective-permute-start.9 = (bf16[128,1024]{1,0:T(8,128)(2,1)S(1)}, bf16[128,1024]{1,0:T(8,128)(2,1)S(1)}, u32[]{:S(2)}, u32[]{:S(2)}) collective-permute-start(bf16[128,1024]{1,0:T(8,128)(2,1)S(1)} %get-tuple-element.37), channel_id=1, source_target_pairs={{0,3},{1,2},{2,1},{3,0},{4,7},{5,6},{6,5},{7,4},{8,11},{9,10},{10,... | collective-permute-start | bytes 786440 | tf_op jit(solution)/shard_map/ppermute | solution.py:23
  14.4 0.7 copy-start.8
  16.9 2.3 %copy-start = (f32[2048,640]{1,0:T(8,128)}, f32[2048,640]{1,0:T(8,128)S(1)}, u32[]{:S(2)}) copy-start(f32[2048,640]{1,0:T(8,128)S(1)} %bias_tiles.1.bias_ref) | copy-start | bytes 15728644
  19.3 13.7 %collective-permute-start.4 = (bf16[128,1024]{1,0:T(8,128)(2,1)S(1)}, bf16[128,1024]{1,0:T(8,128)(2,1)S(1)}, u32[]{:S(2)}, u32[]{:S(2)}) collective-permute-start(bf16[128,1024]{1,0:T(8,128)(2,1)S(1)} %collective-permute-done.3.s0), channel_id=1, source_target_pairs={{0,1},{1,0},{2,3},{3,2},{4,5},{5,4},{6,7},{7,6},{8,9},{9,8},{10,11... | collective-permute-start | bytes 786440 | tf_op jit(solution)/shard_map/ppermute | solution.py:23
  24.1 12.5 %collective-permute-start.6 = (bf16[128,1024]{1,0:T(8,128)(2,1)S(1)}, bf16[128,1024]{1,0:T(8,128)(2,1)S(1)}, u32[]{:S(2)}, u32[]{:S(2)}) collective-permute-start(bf16[128,1024]{1,0:T(8,128)(2,1)S(1)} %collective-permute-done.5.s1), channel_id=1, source_target_pairs={{0,1},{1,0},{2,3},{3,2},{4,5},{5,4},{6,7},{7,6},{8,9},{9,8},{10,11... | collective-permute-start | bytes 786440 | tf_op jit(solution)/shard_map/ppermute | solution.py:23
  26.8 15.9 %slice-start = ((s8[5242880]{0:T(1024)(128)(4,1)}), s8[4194304]{0:T(1024)(128)(4,1)S(1)}, s32[]{:S(2)}) async-start(s8[5242880]{0:T(1024)(128)(4,1)} %bitcast.8), calls=%async_computation | async-start | bytes 8388608
  36.6 6.2 %slice-start.1 = ((s8[5242880]{0:T(1024)(128)(4,1)}), s8[1048576]{0:T(1024)(128)(4,1)S(1)}, s32[]{:S(2)}) async-start(s8[5242880]{0:T(1024)(128)(4,1)} %bitcast.8), calls=%async_computation.1 | async-start | bytes 2097152
  36.6 6.2 %copy-start.1 = (bf16[1024,2048]{1,0:T(8,128)(2,1)S(1)}, bf16[1024,2048]{1,0:T(8,128)(2,1)}, u32[]{:S(2)}) copy-start(bf16[1024,2048]{1,0:T(8,128)(2,1)} %w_ref.3) | copy-start | bytes 12582916
  36.6 6.2 %copy-start.6 = (s32[512]{0:T(512)S(1)}, s32[512]{0:T(512)}, u32[]{:S(2)}) copy-start(s32[512]{0:T(512)} %seg_ref.3) | copy-start | bytes 6148
  48.8 13.9 %collective-permute-start.11 = (bf16[256,1024]{1,0:T(8,128)(2,1)S(1)}, bf16[256,1024]{1,0:T(8,128)(2,1)S(1)}, u32[]{:S(2)}, u32[]{:S(2)}) collective-permute-start(bf16[256,1024]{1,0:T(8,128)(2,1)S(1)} %get-tuple-element.49), channel_id=1, source_target_pairs={{0,1},{1,0},{2,3},{3,2},{4,5},{5,4},{6,7},{7,6},{8,9},{9,8},{10,11... | collective-permute-start | bytes 1572872 | tf_op jit(solution)/shard_map/ppermute | solution.py:23
  49.2 41.1 %copy-start.3 = (bf16[2048,1024]{1,0:T(8,128)(2,1)S(1)}, bf16[2048,1024]{1,0:T(8,128)(2,1)}, u32[]{:S(2)}) copy-start(bf16[2048,1024]{1,0:T(8,128)(2,1)} %wv.7) | copy-start | bytes 12582916
  55.2 35.1 %copy-start.2 = (bf16[2048,1024]{1,0:T(8,128)(2,1)S(1)}, bf16[2048,1024]{1,0:T(8,128)(2,1)}, u32[]{:S(2)}) copy-start(bf16[2048,1024]{1,0:T(8,128)(2,1)} %wk.7) | copy-start | bytes 12582916
  55.2 35.1 %copy-start.7 = (f32[2048]{0:T(1024)S(1)}, f32[2048]{0:T(1024)}, u32[]{:S(2)}) copy-start(f32[2048]{0:T(1024)} %param.23) | copy-start | bytes 24580
  55.2 18.8 %collective-permute-start.10 = (bf16[256,1024]{1,0:T(8,128)(2,1)S(1)}, bf16[256,1024]{1,0:T(8,128)(2,1)S(1)}, u32[]{:S(2)}, u32[]{:S(2)}) collective-permute-start(bf16[256,1024]{1,0:T(8,128)(2,1)S(1)} %get-tuple-element.46), channel_id=1, source_target_pairs={{0,1},{1,0},{2,3},{3,2},{4,5},{5,4},{6,7},{7,6},{8,9},{9,8},{10,11... | collective-permute-start | bytes 1572872 | tf_op jit(solution)/shard_map/ppermute | solution.py:23
  64.3 13.6 %collective-permute-start.12 = (bf16[128,1024]{1,0:T(8,128)(2,1)S(1)}, bf16[128,1024]{1,0:T(8,128)(2,1)S(1)}, u32[]{:S(2)}, u32[]{:S(2)}) collective-permute-start(bf16[128,1024]{1,0:T(8,128)(2,1)S(1)} %get-tuple-element.52), channel_id=1, source_target_pairs={{0,5},{1,4},{2,7},{3,6},{4,1},{5,0},{6,3},{7,2},{8,13},{9,12},{10,... | collective-permute-start | bytes 786440 | tf_op jit(solution)/shard_map/ppermute | solution.py:23
  64.3 14.9 %collective-permute-start.14 = (bf16[128,1024]{1,0:T(8,128)(2,1)S(1)}, bf16[128,1024]{1,0:T(8,128)(2,1)S(1)}, u32[]{:S(2)}, u32[]{:S(2)}) collective-permute-start(bf16[128,1024]{1,0:T(8,128)(2,1)S(1)} %get-tuple-element.53), channel_id=1, source_target_pairs={{0,7},{1,6},{2,5},{3,4},{4,3},{5,2},{6,1},{7,0},{8,15},{9,14},{10,... | collective-permute-start | bytes 786440 | tf_op jit(solution)/shard_map/ppermute | solution.py:23
  75.5 3.8 %collective-permute-start.16 = (bf16[128,1024]{1,0:T(8,128)(2,1)S(1)}, bf16[128,1024]{1,0:T(8,128)(2,1)S(1)}, u32[]{:S(2)}, u32[]{:S(2)}) collective-permute-start(bf16[128,1024]{1,0:T(8,128)(2,1)S(1)} %get-tuple-element.55), channel_id=1, source_target_pairs={{0,2},{1,3},{2,0},{3,1},{4,6},{5,7},{6,4},{7,5},{8,10},{9,11},{10,... | collective-permute-start | bytes 786440 | tf_op jit(solution)/shard_map/ppermute | solution.py:23
  76.2 7.9 %collective-permute-start.17 = (bf16[128,1024]{1,0:T(8,128)(2,1)S(1)}, bf16[128,1024]{1,0:T(8,128)(2,1)S(1)}, u32[]{:S(2)}, u32[]{:S(2)}) collective-permute-start(bf16[128,1024]{1,0:T(8,128)(2,1)S(1)} %get-tuple-element.54.f0), channel_id=1, source_target_pairs={{0,1},{1,0},{2,3},{3,2},{4,5},{5,4},{6,7},{7,6},{8,9},{9,8},{10,11... | collective-permute-start | bytes 786440 | tf_op jit(solution)/shard_map/ppermute | solution.py:23
  76.3 14.0 %collective-permute-start.18 = (bf16[128,1024]{1,0:T(8,128)(2,1)S(1)}, bf16[128,1024]{1,0:T(8,128)(2,1)S(1)}, u32[]{:S(2)}, u32[]{:S(2)}) collective-permute-start(bf16[128,1024]{1,0:T(8,128)(2,1)S(1)} %get-tuple-element.55), channel_id=1, source_target_pairs={{0,3},{1,2},{2,1},{3,0},{4,7},{5,6},{6,5},{7,4},{8,11},{9,10},{10,... | collective-permute-start | bytes 786440 | tf_op jit(solution)/shard_map/ppermute | solution.py:23
  77.8 18.4 %collective-permute-start.13 = (bf16[128,1024]{1,0:T(8,128)(2,1)S(1)}, bf16[128,1024]{1,0:T(8,128)(2,1)S(1)}, u32[]{:S(2)}, u32[]{:S(2)}) collective-permute-start(bf16[128,1024]{1,0:T(8,128)(2,1)S(1)} %collective-permute-done.12.s0), channel_id=1, source_target_pairs={{0,1},{1,0},{2,3},{3,2},{4,5},{5,4},{6,7},{7,6},{8,9},{9,8},{10,11... | collective-permute-start | bytes 786440 | tf_op jit(solution)/shard_map/ppermute | solution.py:23
  79.1 21.9 %collective-permute-start.15 = (bf16[128,1024]{1,0:T(8,128)(2,1)S(1)}, bf16[128,1024]{1,0:T(8,128)(2,1)S(1)}, u32[]{:S(2)}, u32[]{:S(2)}) collective-permute-start(bf16[128,1024]{1,0:T(8,128)(2,1)S(1)} %collective-permute-done.14.s1), channel_id=1, source_target_pairs={{0,1},{1,0},{2,3},{3,2},{4,5},{5,4},{6,7},{7,6},{8,9},{9,8},{10,11... | collective-permute-start | bytes 786440 | tf_op jit(solution)/shard_map/ppermute | solution.py:23
